TPU v7x, 32 devices: a whole 2x2x4 slice. The times are simulated.
32 devices in a mesh: req: 4 (over y, x), mlp: 8 (over z, core).
Axes of the slice: x: 2, y: 2, z: 4, core: 2. Of those that a mesh axis runs over, the one named last changes fastest.
Arguments:
- tokens: bfloat16 [64, 4608], P(('req', 'mlp')), may hold values from -6 to 6
- segments: int32 [4, 16], replicated, may hold values from 0 to 3, never falling along the last dimension, each value on 1 to 8 neighbouring positions
- owners: int32 [4], replicated, may hold values from 0 to 3, each once
- sink_keys: bfloat16 [4, 2048], P(None, 'mlp'), may hold values from -21 to 21
- sink_values: bfloat16 [4, 2048], P(None, 'mlp'), may hold values from -6 to 6
- window_keys: bfloat16 [4096, 2048], P('req', 'mlp'), may hold values from -6 to 6
- window_values: bfloat16 [4096, 2048], P('req', 'mlp'), may hold values from -6 to 6
- attn_gain: float32 [4608], replicated, may hold values from 0.1 to 1.9
- post_attn_gain: float32 [4608], replicated, may hold values from 0.1 to 1.9
- ffn_gain: float32 [4608], replicated, may hold values from 0.1 to 1.9
- post_ffn_gain: float32 [4608], replicated, may hold values from 0.1 to 1.9
- w_query: bfloat16 [4608, 4096], P(None, 'mlp'), may hold values from -0.09375 to 0.09375
- w_key: bfloat16 [4608, 2048], P(None, 'mlp'), may hold values from -0.25 to 0.25
- w_value: bfloat16 [4608, 2048], P(None, 'mlp'), may hold values from -0.09375 to 0.09375
- w_out: bfloat16 [4096, 4608], P('mlp'), may hold values from -0.09375 to 0.09375
- w_gate: bfloat16 [36864, 4608], P(('req', 'mlp')), may hold values from -0.09375 to 0.09375
- w_up: bfloat16 [36864, 4608], P(('req', 'mlp')), may hold values from -0.09375 to 0.09375
- w_down: bfloat16 [36864, 4608], P(('req', 'mlp')), may hold values from -0.03125 to 0.03125
Outputs:
- mixed: bfloat16 [64, 4608], P(('req', 'mlp'))
Inputs may be any that keep to these rules, and one draw needn't show every extreme that they name: `segments`: row g gives, for the 16 suffix tokens of request group g in order, which of the group's 4 requests each belongs to; a request's tokens are contiguous and its number never falls along the row. Req index d holds array rows d * B to d * B + B - 1 of window_keys and window_values, whose window positions are owners[d] * B to owners[d] * B + B - 1, B = 4096 / 4; every block of positions is held once.
All inputs are finite; a program needn't handle non-finite values.
Results may differ from a plain program's by a relative error of at most 0.015.
Values may be sent and summed in bfloat16 or wider, within the bound.
A program may use at most 128 MiB of HBM per device.

v0:
```python
import jax
import jax.numpy as jnp
from jax import lax
from jax.sharding import PartitionSpec as P

HEADS = 32
KVH = 16
HD = 128
SINK = 4
GTOK = 16
epsilon = 1e-06
soft_cap = 50.0
logit_scale = 1.0 / 12.0


def rms_scale(values):
    return values * lax.rsqrt(jnp.mean(values * values, axis=-1, keepdims=True) + epsilon)


def positions(seg_rows):
    ordering = jnp.arange(seg_rows.shape[-1], dtype=jnp.int32)
    same_seg = seg_rows[..., :, None] == seg_rows[..., None, :]
    earlier = ordering[None, :] < ordering[:, None]
    return jnp.sum((same_seg & earlier).astype(jnp.int32), axis=-1)


def lookup(entries, indices):
    slots = jnp.arange(entries.shape[0], dtype=jnp.int32)
    return jnp.sum(jnp.where(indices[:, None] == slots[None, :], entries[None, :], 0), axis=1)


def attend(query_rows, key_matrix_rows, value_matrix_rows, visible):
    score_matrix = (
        jnp.einsum(
            "woji,roi->wojr", query_rows, key_matrix_rows, preferred_element_type=jnp.float32
        )
        * logit_scale
    )
    weight = jnp.exp(soft_cap * jnp.tanh(score_matrix / soft_cap))
    weight = jnp.where(visible[:, None, None, :], weight, 0.0)
    totals = jnp.sum(weight, axis=-1)
    summed_output = jnp.einsum(
        "xfka,afq->xfkq",
        weight.astype(jnp.bfloat16),
        value_matrix_rows,
        preferred_element_type=jnp.float32,
    )
    return (summed_output, totals)


def shards(
    tokens,
    segments,
    owners,
    sink_keys,
    sink_values,
    window_keys,
    window_values,
    attn_gain,
    post_attn_gain,
    ffn_gain,
    post_ffn_gain,
    w_query,
    w_key,
    w_value,
    w_out,
    w_gate,
    w_up,
    w_down,
):
    per_kv = HEADS // KVH
    local_heads = w_key.shape[1] // HD
    token_float = tokens.astype(jnp.float32)
    normed = (rms_scale(token_float) * attn_gain).astype(jnp.bfloat16)
    group_rows = lax.all_gather(normed, "mlp", axis=0, tiled=True)
    query_rows = (
        jnp.dot(group_rows, w_query, preferred_element_type=jnp.float32)
        .astype(jnp.bfloat16)
        .reshape(GTOK, local_heads, per_kv, HD)
    )
    key_new = (
        jnp.dot(group_rows, w_key, preferred_element_type=jnp.float32)
        .astype(jnp.bfloat16)
        .reshape(GTOK, local_heads, HD)
    )
    value_new = (
        jnp.dot(group_rows, w_value, preferred_element_type=jnp.float32)
        .astype(jnp.bfloat16)
        .reshape(GTOK, local_heads, HD)
    )
    req_index = lax.axis_index("req")
    pos_all = positions(segments)
    pos_row = lax.dynamic_index_in_dim(pos_all, req_index, 0, keepdims=False)
    seg_row = lax.dynamic_index_in_dim(segments, req_index, 0, keepdims=False)
    sink_key = sink_keys.reshape(SINK, local_heads, HD)
    sink_value = sink_values.reshape(SINK, local_heads, HD)
    sink_sum, sink_tot = attend(
        query_rows, sink_key, sink_value, jnp.ones((GTOK, SINK), dtype=jnp.bool_)
    )
    ordering = jnp.arange(GTOK, dtype=jnp.int32)
    local_vis = (seg_row[:, None] == seg_row[None, :]) & (ordering[None, :] <= ordering[:, None])
    loc_sum, loc_tot = attend(query_rows, key_new, value_new, local_vis)
    block_rows = window_keys.shape[0]
    piece_key = lax.all_gather(window_keys, "req", axis=0, tiled=True).reshape(-1, local_heads, HD)
    piece_value = lax.all_gather(window_values, "req", axis=0, tiled=True).reshape(
        -1, local_heads, HD
    )
    row_ids = jnp.arange(piece_key.shape[0], dtype=jnp.int32)
    window_pos = lookup(owners, row_ids // block_rows) * block_rows + row_ids % block_rows
    part_sum, part_tot = attend(
        query_rows, piece_key, piece_value, window_pos[None, :] > pos_row[:, None]
    )
    merged = (sink_sum + part_sum + loc_sum) / (sink_tot + part_tot + loc_tot)[..., None]
    attended = merged.astype(jnp.bfloat16).reshape(GTOK, local_heads * per_kv * HD)
    projected = jnp.dot(attended, w_out, preferred_element_type=jnp.float32)
    head_total = lax.psum_scatter(
        projected.astype(jnp.bfloat16), "mlp", scatter_dimension=0, tiled=True
    ).astype(jnp.float32)
    residual = token_float + rms_scale(head_total) * post_attn_gain
    ffn_in = (rms_scale(residual) * ffn_gain).astype(jnp.bfloat16)
    contract = (((1,), (1,)), ((), ()))
    piece = lax.all_gather(ffn_in, ("req", "mlp"), axis=0, tiled=True)
    gate_part = lax.dot_general(piece, w_gate, contract, preferred_element_type=jnp.float32)
    up_part = lax.dot_general(piece, w_up, contract, preferred_element_type=jnp.float32)
    hidden = (jax.nn.gelu(gate_part, approximate=True) * up_part).astype(jnp.bfloat16)
    ffn_out = lax.psum_scatter(
        jnp.dot(hidden, w_down, preferred_element_type=jnp.float32),
        ("req", "mlp"),
        scatter_dimension=0,
        tiled=True,
    )
    return (residual + rms_scale(ffn_out) * post_ffn_gain).astype(jnp.bfloat16)


def solution(mesh):
    return jax.shard_map(
        shards,
        mesh=mesh,
        in_specs=(
            P(("req", "mlp"), None),
            P(),
            P(),
            P(None, "mlp"),
            P(None, "mlp"),
            P("req", "mlp"),
            P("req", "mlp"),
            P(),
            P(),
            P(),
            P(),
            P(None, "mlp"),
            P(None, "mlp"),
            P(None, "mlp"),
            P("mlp", None),
            P(("req", "mlp"), None),
            P(("req", "mlp"), None),
            P(("req", "mlp"), None),
        ),
        out_specs=P(("req", "mlp"), None),
        check_vma=False,
    )
```

profile of v0, /device:TPU:0, one launch (start us, length us, event | category | flops | bytes accessed | tf_op | source)
XLA Modules:
  0.0 348.4 jit_solution(10756203467283247268)
XLA Ops:
  6.5 2.2 copy.56
  8.8 2.0 copy.59
  10.9 0.9 fusion.36
  11.8 0.8 fusion.43
  12.7 15.7 %all-gather = bf16[8,2,4608]{2,1,0:T(2,128)(2,1)S(1)} all-gather(bf16[1,2,4608]{2,1,0:T(2,128)(2,1)S(1)} %fusion.43), channel_id=1, replica_groups=mesh['req'=4,'mlp'=8] {'mlp'}, dimensions={0}, use_global_device_ids=true | all-gather | bytes 165888 | tf_op jit(solution)/shard_map/all_gather | solution.py:75
  28.5 3.1 convolution_convert_fusion.1
  31.6 0.4 convolution_convert_fusion.2
  32.0 2.1 convolution_convert_fusion.3
  35.1 12.1 %all-gather.5.cloned.1.call-done = bf16[4096,256]{0,1:T(8,128)(2,1)} async-done(((bf16[1024,256]{0,1:T(8,128)(2,1)}), bf16[4096,256]{0,1:T(8,128)(2,1)}) %all-gather.5.cloned.1.call-update) | async-done | bytes 2097168 | tf_op jit(solution)/shard_map/all_gather | solution.py:104
  47.3 2.3 fusion.65
  49.6 34.9 %all-gather.7.cloned.1.call-done = bf16[4096,256]{0,1:T(8,128)(2,1)} async-done(((bf16[1024,256]{0,1:T(8,128)(2,1)}), bf16[4096,256]{0,1:T(8,128)(2,1)}) %all-gather.7.cloned.1.call-update) | async-done | bytes 2097168 | tf_op jit(solution)/shard_map/all_gather | solution.py:105
  84.4 2.4 fusion.20
  87.3 3.7 %convolution_convert_fusion = bf16[16,4608]{1,0:T(8,128)(2,1)} fusion(bf16[16,512]{1,0:T(8,128)(2,1)S(1)} %reshape.183, bf16[512,4608]{1,0:T(8,128)(2,1)} %param.32), kind=kOutput, calls=%fused_computation | convolution fusion | flops 75571200 | bytes 4882432 | tf_op jit(solution)/shard_map/dot_general | solution.py:115
  91.1 0.6 dynamic-slice
  92.3 51.0 %all-reduce.5.cloned.1.call-done = bf16[16,4608]{1,0:T(8,128)(2,1)} async-done(((bf16[16,4608]{1,0:T(8,128)(2,1)}), bf16[16,4608]{1,0:T(8,128)(2,1)}) %all-reduce.5.cloned.1.call-update) | async-done | bytes 147472
  143.3 1.0 fusion.34
  144.4 1.1 multiply_reduce_fusion.1
  145.6 0.5 copy-done.1
  146.1 44.4 %all-gather.1 = bf16[32,2,4608]{2,1,0:T(2,128)(2,1)S(1)} all-gather(bf16[1,2,4608]{2,1,0:T(2,128)(2,1)S(1)} %fusion.44), channel_id=1, replica_groups=mesh['req'=4,'mlp'=8] {'req','mlp'}, dimensions={0}, use_global_device_ids=true | all-gather | bytes 608256 | tf_op jit(solution)/shard_map/all_gather | solution.py:122
  190.7 7.3 %fusion.66 = f32[64,1152]{1,0:T(8,128)S(1)} fusion(bf16[64,4608]{1,0:T(8,128)(2,1)S(1)} %reshape.187, bf16[1152,4608]{1,0:T(8,128)(2,1)} %param.33), kind=kOutput, calls=%fused_computation.102 | convolution fusion | flops 679477248 | bytes 11501568 | tf_op jit(solution)/shard_map/dot_general | solution.py:123
  198.1 13.6 %fusion.19 = f32[64,4608]{1,0:T(8,128)} fusion(bf16[1152,4608]{1,0:T(8,128)(2,1)} %param.35, bf16[64,4608]{1,0:T(8,128)(2,1)S(1)} %reshape.187, bf16[1152,4608]{1,0:T(8,128)(2,1)} %param.34, f32[64,1152]{1,0:T(8,128)S(1)} %fusion.66), kind=kOutput, calls=%fused_computation.29 | convolution fusion | flops 1359691776 | bytes 23298048 | tf_op jit(solution)/shard_map/dot_general | solution.py:127
  211.7 127.5 %all-reduce.7.cloned.1.call-done = f32[64,4608]{1,0:T(8,128)} async-done(((f32[64,4608]{1,0:T(8,128)}), f32[64,4608]{1,0:T(8,128)}) %all-reduce.7.cloned.1.call-update) | async-done | bytes 1179664
  339.2 1.1 multiply_reduce_fusion
  340.3 1.6 add_convert_fusion
  (57 shorter events, 2.0 us)
Async XLA Ops:
  6.5 25.0 %copy-start = (bf16[4608,256]{1,0:T(8,128)(2,1)S(1)}, bf16[4608,256]{1,0:T(8,128)(2,1)}, u32[]{:S(2)}) copy-start(bf16[4608,256]{1,0:T(8,128)(2,1)} %param.30) | copy-start | bytes 7077892
  6.5 40.7 %all-gather.5.cloned.1.call-start = ((), (), s32[]{:S(2)}) async-start(), calls=%async_computation | async-start | bytes 2621440 | tf_op jit(solution)/shard_map/all_gather | solution.py:104
  8.8 75.7 %all-gather.7.cloned.1.call-start = ((), (), s32[]{:S(2)}) async-start(), calls=%async_computation.1 | async-start | bytes 2621440 | tf_op jit(solution)/shard_map/all_gather | solution.py:105
  10.9 132.4 %all-reduce.5.cloned.1.call-start = ((), (), s32[]{:S(2)}) async-start(), calls=%async_computation.2 | async-start | bytes 294912
  28.5 5.7 %copy-start.7 = (s32[4,16]{1,0:T(4,128)S(1)}, s32[4,16]{1,0:T(4,128)}, u32[]{:S(2)}) copy-start(s32[4,16]{1,0:T(4,128)} %param.19) | copy-start | bytes 772
  28.5 5.9 %copy-start.9 = (s32[4]{0:T(128)S(1)}, s32[4]{0:T(128)}, u32[]{:S(2)}) copy-start(s32[4]{0:T(128)} %param.20) | copy-start | bytes 52
  28.5 6.1 %copy-start.10 = (bf16[4,256]{1,0:T(4,128)(2,1)S(1)}, bf16[4,256]{1,0:T(4,128)(2,1)}, u32[]{:S(2)}) copy-start(bf16[4,256]{1,0:T(4,128)(2,1)} %param.21) | copy-start | bytes 6148
  32.0 54.9 %copy-start.8 = (bf16[4,256]{1,0:T(4,128)(2,1)S(1)}, bf16[4,256]{1,0:T(4,128)(2,1)}, u32[]{:S(2)}) copy-start(bf16[4,256]{1,0:T(4,128)(2,1)} %param.22) | copy-start | bytes 6148
  49.5 41.5 %copy-start.11 = (u32[32]{0:T(128)S(1)}, u32[32]{0:T(128)}, u32[]{:S(2)}) copy-start(u32[32]{0:T(128)} %constant.81) | copy-start | bytes 388
  49.6 94.8 %copy-start.3 = (bf16[2,4608]{1,0:T(2,128)(2,1)S(1)}, bf16[2,4608]{1,0:T(2,128)(2,1)}, u32[]{:S(2)}) copy-start(bf16[2,4608]{1,0:T(2,128)(2,1)} %param.18) | copy-start | bytes 55300
  49.6 94.8 %copy-start.5 = (f32[4608]{0:T(1024)S(1)}, f32[4608]{0:T(1024)}, u32[]{:S(2)}) copy-start(f32[4608]{0:T(1024)} %param.26) | copy-start | bytes 55300
  49.6 95.9 %copy-start.6 = (f32[4608]{0:T(1024)S(1)}, f32[4608]{0:T(1024)}, u32[]{:S(2)}) copy-start(f32[4608]{0:T(1024)} %param.27) | copy-start | bytes 55300
  91.0 248.1 %all-reduce.7.cloned.1.call-start = ((), (), s32[]{:S(2)}) async-start(), calls=%async_computation.3 | async-start | bytes 2359296
  145.5 0.6 copy-start.1
  198.0 142.2 %copy-start.2 = (f32[2,4608]{1,0:T(2,128)S(1)}, f32[2,4608]{1,0:T(2,128)}, u32[]{:S(2)}) copy-start(f32[2,4608]{1,0:T(2,128)} %copy-done.1) | copy-start | bytes 110596
  198.0 142.2 %copy-start.4 = (f32[4608]{0:T(1024)S(1)}, f32[4608]{0:T(1024)}, u32[]{:S(2)}) copy-start(f32[4608]{0:T(1024)} %param.28) | copy-start | bytes 55300
Sparse Core Ops, SparseCore 0:
  9.2 38.0 all-gather.4
  49.1 35.2 all-gather.6
  91.2 52.0 all-reduce.4
  211.8 127.3 all-reduce.6
where the time goes:
time: 349 us; the launch traced here: 348 us
  waiting for transfers between devices  225 us (64%)
  blocking collectives  60.1 us (17%)
  matrix products  35.6 us (10%)
  between operations  14 us (4%)
  other arithmetic  7.19 us (2%)
  local copies, waits for them, and re-layouts  5.76 us (2%)
    unnamed x6, waiting for transfers between devices  178 us
    all_gather x1, blocking collectives, shards(): piece = lax.all_gather(ffn_in, ('req', 'mlp'), axis=0, tiled=True)  44.4 us
    all_gather x1, waiting for transfers between devices, shards(): lax.all_gather(window_values, 'req', axis=0, tiled=True)  34.9 us
    all_gather x1, blocking collectives, shards(): group_rows = lax.all_gather(normed, 'mlp', axis=0, tiled=True)  15.7 us
    dot_general x1, matrix products, shards(): jnp.dot(hidden, w_down, preferred_element_type=jnp.float32)  13.6 us
    all_gather x1, waiting for transfers between devices, shards(): lax.all_gather(window_keys, 'req', axis=0, tiled=True)  12.1 us
    dot_general x1, matrix products, shards(): lax.dot_general(piece, w_gate, contract, preferred_element_type=jnp.float32)  7.31 us
  transfers between devices with their start and end apart: 4, of which 4 were waited for; matrix products, arithmetic and copies ran while one was open for 4% of the time, Pallas kernels for 0%

commit v1 on v0

--- a/solution.py
+++ b/solution.py
@@ -2,6 +2,7 @@
 import jax.numpy as jnp
 from jax import lax
 from jax.sharding import PartitionSpec as P
+from jax.lax import axis_index, ppermute, psum
 
 HEADS = 32
 KVH = 16
@@ -72,7 +73,21 @@
     local_heads = w_key.shape[1] // HD
     token_float = tokens.astype(jnp.float32)
     normed = (rms_scale(token_float) * attn_gain).astype(jnp.bfloat16)
-    group_rows = lax.all_gather(normed, "mlp", axis=0, tiled=True)
+
+    def frames_open(sample, across):
+        n_chips = psum(1, axis_name=across)
+        next_value = sample
+        local_next = sorted(((src_i, (src_i + 1) % n_chips) for src_i in range(n_chips)))
+        row_list = [next_value]
+        for pp in range(1, n_chips):
+            next_value = ppermute(next_value, axis_name=across, perm=local_next)
+            row_list.insert(0, next_value)
+        latest = jnp.concatenate(row_list, axis=0)
+        new = axis_index(across)
+        small = new + 1
+        return jnp.roll(latest, small * sample.shape[0], axis=0)
+
+    group_rows = frames_open(normed, "mlp")
     query_rows = (
         jnp.dot(group_rows, w_query, preferred_element_type=jnp.float32)
         .astype(jnp.bfloat16)

time: 349 us -> 349 us (level)
  blocking collectives: 60.1 us -> 44.4 us
  waiting for transfers between devices: 225 us -> 238 us
    ppermute x0 -> x7, waiting for transfers between devices: none -> 30.4 us  [frames_open(): next_value = ppermute(next_value, axis_name=across, perm=local_next)]
    all_gather x1 -> x0, blocking collectives: 15.7 us -> none  [shards(): group_rows = lax.all_gather(normed, 'mlp', axis=0, tiled=True)]
    all_gather x1, waiting for transfers between devices: 12.1 us -> 0.02 us  [shards(): lax.all_gather(window_keys, 'req', axis=0, tiled=True)]
    all_gather x1, waiting for transfers between devices: 34.9 us -> 29.2 us  [shards(): lax.all_gather(window_values, 'req', axis=0, tiled=True)]
  transfers between devices with their start and end apart: 4 -> 11, of which waited for: 4 -> 10; matrix products, arithmetic and copies ran while one was open for 4% -> 5% of each run, Pallas kernels for 0% -> 0%
where the time goes in v1:
time: 349 us
  waiting for transfers between devices  238 us (68%)
  blocking collectives  44.4 us (13%)
  matrix products  35.7 us (10%)
  between operations  14 us (4%)
  other arithmetic  8.61 us (2%)
  local copies, waits for them, and re-layouts  6.8 us (2%)
    unnamed x6, waiting for transfers between devices  179 us
    all_gather x1, blocking collectives, shards(): piece = lax.all_gather(ffn_in, ('req', 'mlp'), axis=0, tiled=True)  44.4 us
    ppermute x7, waiting for transfers between devices, frames_open(): next_value = ppermute(next_value, axis_name=across, perm=local_next)  30.4 us
    all_gather x1, waiting for transfers between devices, shards(): lax.all_gather(window_values, 'req', axis=0, tiled=True)  29.2 us
    dot_general x1, matrix products, shards(): jnp.dot(hidden, w_down, preferred_element_type=jnp.float32)  13.6 us
    dot_general x1, matrix products, shards(): lax.dot_general(piece, w_gate, contract, preferred_element_type=jnp.float32)  7.32 us
  transfers between devices with their start and end apart: 11, of which 10 were waited for; matrix products, arithmetic and copies ran while one was open for 5% of the time, Pallas kernels for 0%

profile of v1, /device:TPU:0, one launch (start us, length us, event | category | flops | bytes accessed | tf_op | source)
XLA Modules:
  0.0 348.5 jit_solution(3159331643518075505)
XLA Ops:
  6.5 2.2 copy.56
  11.1 2.0 copy.59
  14.0 2.6 collective-permute-done
  16.7 4.8 %collective-permute-done.1 = bf16[2,4608]{1,0:T(2,128)(2,1)S(1)} collective-permute-done((bf16[2,4608]{1,0:T(2,128)(2,1)S(1)}, bf16[2,4608]{1,0:T(2,128)(2,1)S(1)}, u32[]{:S(2)}, u32[]{:S(2)}) %collective-permute-start.1) | collective-permute-done | bytes 18464 | tf_op jit(solution)/shard_map/ppermute | solution.py:83
  22.5 4.0 %collective-permute-done.2 = bf16[2,4608]{1,0:T(2,128)(2,1)S(1)} collective-permute-done((bf16[2,4608]{1,0:T(2,128)(2,1)S(1)}, bf16[2,4608]{1,0:T(2,128)(2,1)S(1)}, u32[]{:S(2)}, u32[]{:S(2)}) %collective-permute-start.2) | collective-permute-done | bytes 18464 | tf_op jit(solution)/shard_map/ppermute | solution.py:83
  26.5 5.0 %collective-permute-done.3 = bf16[2,4608]{1,0:T(2,128)(2,1)S(1)} collective-permute-done((bf16[2,4608]{1,0:T(2,128)(2,1)S(1)}, bf16[2,4608]{1,0:T(2,128)(2,1)S(1)}, u32[]{:S(2)}, u32[]{:S(2)}) %collective-permute-start.3) | collective-permute-done | bytes 18464 | tf_op jit(solution)/shard_map/ppermute | solution.py:83
  31.6 4.9 %collective-permute-done.4 = bf16[2,4608]{1,0:T(2,128)(2,1)S(1)} collective-permute-done((bf16[2,4608]{1,0:T(2,128)(2,1)S(1)}, bf16[2,4608]{1,0:T(2,128)(2,1)S(1)}, u32[]{:S(2)}, u32[]{:S(2)}) %collective-permute-start.4) | collective-permute-done | bytes 18464 | tf_op jit(solution)/shard_map/ppermute | solution.py:83
  37.2 4.3 %collective-permute-done.5 = bf16[2,4608]{1,0:T(2,128)(2,1)S(1)} collective-permute-done((bf16[2,4608]{1,0:T(2,128)(2,1)S(1)}, bf16[2,4608]{1,0:T(2,128)(2,1)S(1)}, u32[]{:S(2)}, u32[]{:S(2)}) %collective-permute-start.5) | collective-permute-done | bytes 18464 | tf_op jit(solution)/shard_map/ppermute | solution.py:83
  41.5 4.9 %collective-permute-done.6 = bf16[2,4608]{1,0:T(2,128)(2,1)S(1)} collective-permute-done((bf16[2,4608]{1,0:T(2,128)(2,1)S(1)}, bf16[2,4608]{1,0:T(2,128)(2,1)S(1)}, u32[]{:S(2)}, u32[]{:S(2)}) %collective-permute-start.6) | collective-permute-done | bytes 18464 | tf_op jit(solution)/shard_map/ppermute | solution.py:83
  47.4 3.1 convolution_convert_fusion.1
  50.4 2.1 convolution_convert_fusion.2
  53.0 2.3 fusion.72
  55.3 29.2 %all-gather.6.cloned.1.call-done = bf16[4096,256]{0,1:T(8,128)(2,1)} async-done(((bf16[1024,256]{0,1:T(8,128)(2,1)}), bf16[4096,256]{0,1:T(8,128)(2,1)}) %all-gather.6.cloned.1.call-update) | async-done | bytes 2097168 | tf_op jit(solution)/shard_map/all_gather | solution.py:120
  84.5 2.4 fusion.20
  87.3 3.7 %convolution_convert_fusion = bf16[16,4608]{1,0:T(8,128)(2,1)} fusion(bf16[16,512]{1,0:T(8,128)(2,1)S(1)} %reshape.183, bf16[512,4608]{1,0:T(8,128)(2,1)} %param.32), kind=kOutput, calls=%fused_computation | convolution fusion | flops 75571200 | bytes 4882432 | tf_op jit(solution)/shard_map/dot_general | solution.py:130
  92.4 51.0 %all-reduce.5.cloned.1.call-done = bf16[16,4608]{1,0:T(8,128)(2,1)} async-done(((bf16[16,4608]{1,0:T(8,128)(2,1)}), bf16[16,4608]{1,0:T(8,128)(2,1)}) %all-reduce.5.cloned.1.call-update) | async-done | bytes 147472
  143.3 1.0 fusion.37
  144.4 1.1 multiply_reduce_fusion.1
  146.1 44.4 %all-gather = bf16[32,2,4608]{2,1,0:T(2,128)(2,1)S(1)} all-gather(bf16[1,2,4608]{2,1,0:T(2,128)(2,1)S(1)} %fusion.46), channel_id=1, replica_groups=mesh['req'=4,'mlp'=8] {'req','mlp'}, dimensions={0}, use_global_device_ids=true | all-gather | bytes 608256 | tf_op jit(solution)/shard_map/all_gather | solution.py:137
  190.7 7.3 %fusion.73 = f32[64,1152]{1,0:T(8,128)S(1)} fusion(bf16[64,4608]{1,0:T(8,128)(2,1)S(1)} %reshape.185, bf16[1152,4608]{1,0:T(8,128)(2,1)} %param.33), kind=kOutput, calls=%fused_computation.109 | convolution fusion | flops 679477248 | bytes 11501568 | tf_op jit(solution)/shard_map/dot_general | solution.py:138
  198.1 13.6 %fusion.19 = f32[64,4608]{1,0:T(8,128)} fusion(bf16[1152,4608]{1,0:T(8,128)(2,1)} %param.35, bf16[64,4608]{1,0:T(8,128)(2,1)S(1)} %reshape.185, bf16[1152,4608]{1,0:T(8,128)(2,1)} %param.34, f32[64,1152]{1,0:T(8,128)S(1)} %fusion.73), kind=kOutput, calls=%fused_computation.29 | convolution fusion | flops 1359691776 | bytes 23298048 | tf_op jit(solution)/shard_map/dot_general | solution.py:142
  211.7 127.6 %all-reduce.7.cloned.1.call-done = f32[64,4608]{1,0:T(8,128)} async-done(((f32[64,4608]{1,0:T(8,128)}), f32[64,4608]{1,0:T(8,128)}) %all-reduce.7.cloned.1.call-update) | async-done | bytes 1179664
  339.3 1.1 multiply_reduce_fusion
  340.4 1.6 add_convert_fusion
  (66 shorter events, 8.4 us)
Async XLA Ops:
  6.5 40.4 %copy-start = (bf16[4608,256]{1,0:T(8,128)(2,1)S(1)}, bf16[4608,256]{1,0:T(8,128)(2,1)}, u32[]{:S(2)}) copy-start(bf16[4608,256]{1,0:T(8,128)(2,1)} %param.31) | copy-start | bytes 7077892
  6.5 46.4 %all-gather.4.cloned.1.call-start = ((), (), s32[]{:S(2)}) async-start(), calls=%async_computation | async-start | bytes 2621440 | tf_op jit(solution)/shard_map/all_gather | solution.py:119
  8.8 75.7 %all-gather.6.cloned.1.call-start = ((), (), s32[]{:S(2)}) async-start(), calls=%async_computation.1 | async-start | bytes 2621440 | tf_op jit(solution)/shard_map/all_gather | solution.py:120
  10.5 6.0 %collective-permute-start = (bf16[2,4608]{1,0:T(2,128)(2,1)S(1)}, bf16[2,4608]{1,0:T(2,128)(2,1)S(1)}, u32[]{:S(2)}, u32[]{:S(2)}) collective-permute-start(bf16[2,4608]{1,0:T(2,128)(2,1)S(1)} %fusion.41), channel_id=1, source_target_pairs={{0,1},{1,2},{2,3},{3,4},{4,5},{5,6},{6,7},{7,0},{8,9},{9,10},{10,1... | collective-permute-start | bytes 55304 | tf_op jit(solution)/shard_map/ppermute | solution.py:83
  13.1 130.2 %all-reduce.5.cloned.1.call-start = ((), (), s32[]{:S(2)}) async-start(), calls=%async_computation.2 | async-start | bytes 294912
  16.5 5.0 %collective-permute-start.1 = (bf16[2,4608]{1,0:T(2,128)(2,1)S(1)}, bf16[2,4608]{1,0:T(2,128)(2,1)S(1)}, u32[]{:S(2)}, u32[]{:S(2)}) collective-permute-start(bf16[2,4608]{1,0:T(2,128)(2,1)S(1)} %collective-permute-done), channel_id=1, source_target_pairs={{0,1},{1,2},{2,3},{3,4},{4,5},{5,6},{6,7},{7,0},{8,9},{9,10},{10,1... | collective-permute-start | bytes 55304 | tf_op jit(solution)/shard_map/ppermute | solution.py:83
  21.5 5.0 %collective-permute-start.2 = (bf16[2,4608]{1,0:T(2,128)(2,1)S(1)}, bf16[2,4608]{1,0:T(2,128)(2,1)S(1)}, u32[]{:S(2)}, u32[]{:S(2)}) collective-permute-start(bf16[2,4608]{1,0:T(2,128)(2,1)S(1)} %collective-permute-done.1), channel_id=1, source_target_pairs={{0,1},{1,2},{2,3},{3,4},{4,5},{5,6},{6,7},{7,0},{8,9},{9,10},{10,1... | collective-permute-start | bytes 55304 | tf_op jit(solution)/shard_map/ppermute | solution.py:83
  26.5 5.0 %collective-permute-start.3 = (bf16[2,4608]{1,0:T(2,128)(2,1)S(1)}, bf16[2,4608]{1,0:T(2,128)(2,1)S(1)}, u32[]{:S(2)}, u32[]{:S(2)}) collective-permute-start(bf16[2,4608]{1,0:T(2,128)(2,1)S(1)} %collective-permute-done.2), channel_id=1, source_target_pairs={{0,1},{1,2},{2,3},{3,4},{4,5},{5,6},{6,7},{7,0},{8,9},{9,10},{10,1... | collective-permute-start | bytes 55304 | tf_op jit(solution)/shard_map/ppermute | solution.py:83
  31.5 5.0 %collective-permute-start.4 = (bf16[2,4608]{1,0:T(2,128)(2,1)S(1)}, bf16[2,4608]{1,0:T(2,128)(2,1)S(1)}, u32[]{:S(2)}, u32[]{:S(2)}) collective-permute-start(bf16[2,4608]{1,0:T(2,128)(2,1)S(1)} %collective-permute-done.3), channel_id=1, source_target_pairs={{0,1},{1,2},{2,3},{3,4},{4,5},{5,6},{6,7},{7,0},{8,9},{9,10},{10,1... | collective-permute-start | bytes 55304 | tf_op jit(solution)/shard_map/ppermute | solution.py:83
  36.5 5.0 %collective-permute-start.5 = (bf16[2,4608]{1,0:T(2,128)(2,1)S(1)}, bf16[2,4608]{1,0:T(2,128)(2,1)S(1)}, u32[]{:S(2)}, u32[]{:S(2)}) collective-permute-start(bf16[2,4608]{1,0:T(2,128)(2,1)S(1)} %collective-permute-done.4), channel_id=1, source_target_pairs={{0,1},{1,2},{2,3},{3,4},{4,5},{5,6},{6,7},{7,0},{8,9},{9,10},{10,1... | collective-permute-start | bytes 55304 | tf_op jit(solution)/shard_map/ppermute | solution.py:83
  41.5 5.0 %collective-permute-start.6 = (bf16[2,4608]{1,0:T(2,128)(2,1)S(1)}, bf16[2,4608]{1,0:T(2,128)(2,1)S(1)}, u32[]{:S(2)}, u32[]{:S(2)}) collective-permute-start(bf16[2,4608]{1,0:T(2,128)(2,1)S(1)} %collective-permute-done.5), channel_id=1, source_target_pairs={{0,1},{1,2},{2,3},{3,4},{4,5},{5,6},{6,7},{7,0},{8,9},{9,10},{10,1... | collective-permute-start | bytes 55304 | tf_op jit(solution)/shard_map/ppermute | solution.py:83
  46.9 5.6 %copy-start.8 = (bf16[4,256]{1,0:T(4,128)(2,1)S(1)}, bf16[4,256]{1,0:T(4,128)(2,1)}, u32[]{:S(2)}) copy-start(bf16[4,256]{1,0:T(4,128)(2,1)} %param.21) | copy-start | bytes 6148
  50.4 36.5 %copy-start.7 = (bf16[4,256]{1,0:T(4,128)(2,1)S(1)}, bf16[4,256]{1,0:T(4,128)(2,1)}, u32[]{:S(2)}) copy-start(bf16[4,256]{1,0:T(4,128)(2,1)} %param.22) | copy-start | bytes 6148
  55.2 35.9 %copy-start.9 = (u32[32]{0:T(128)S(1)}, u32[32]{0:T(128)}, u32[]{:S(2)}) copy-start(u32[32]{0:T(128)} %constant.108) | copy-start | bytes 388
  55.3 89.1 %copy-start.3 = (bf16[2,4608]{1,0:T(2,128)(2,1)S(1)}, bf16[2,4608]{1,0:T(2,128)(2,1)}, u32[]{:S(2)}) copy-start(bf16[2,4608]{1,0:T(2,128)(2,1)} %param.18) | copy-start | bytes 55300
  55.3 89.1 %copy-start.5 = (f32[4608]{0:T(1024)S(1)}, f32[4608]{0:T(1024)}, u32[]{:S(2)}) copy-start(f32[4608]{0:T(1024)} %param.26) | copy-start | bytes 55300
  55.3 90.2 %copy-start.6 = (f32[4608]{0:T(1024)S(1)}, f32[4608]{0:T(1024)}, u32[]{:S(2)}) copy-start(f32[4608]{0:T(1024)} %param.27) | copy-start | bytes 55300
  91.1 248.2 %all-reduce.7.cloned.1.call-start = ((), (), s32[]{:S(2)}) async-start(), calls=%async_computation.3 | async-start | bytes 2359296
  145.5 0.6 copy-start.1
  198.0 142.3 %copy-start.2 = (f32[2,4608]{1,0:T(2,128)S(1)}, f32[2,4608]{1,0:T(2,128)}, u32[]{:S(2)}) copy-start(f32[2,4608]{1,0:T(2,128)} %copy-done.1) | copy-start | bytes 110596
  198.1 142.3 %copy-start.4 = (f32[4608]{0:T(1024)S(1)}, f32[4608]{0:T(1024)}, u32[]{:S(2)}) copy-start(f32[4608]{0:T(1024)} %param.28) | copy-start | bytes 55300
Sparse Core Ops, SparseCore 0:
  9.2 38.0 all-gather.3
  49.1 35.2 all-gather.5
  91.2 52.0 all-reduce.4
  211.8 127.3 all-reduce.6
